TPU v7x, 512 devices: a whole 4x4x16 slice. The times are simulated.
512 devices in a mesh: row: 16 (over z), col: 32 (over y, x, core).
Axes of the slice: x: 4, y: 4, z: 16, core: 2. Of those that a mesh axis runs over, the one named last changes fastest.
Arguments:
- flow_state: bfloat16 [131072, 256], P(('col', 'row')), may hold values from -6 to 6
- link_state: bfloat16 [65536, 256], P(('row', 'col')), may hold values from -6 to 6
- incidence: bfloat16 [16, 32, 24, 128, 128], P('row', 'col'), may hold values from -0.29882812 to 0.29882812
- tile_flow: int32 [16, 32, 24], P('row', 'col'), may hold values from 0 to 31
- tile_link: int32 [16, 32, 24], P('row', 'col'), may hold values from 0 to 31
- tile_live: int32 [16, 32, 24], P('row', 'col'), may hold values from 0 to 1, as said below
- link_gain: float32 [256], replicated, may hold values from 0.5 to 2
- link_agg_weight: bfloat16 [256, 256], replicated, may hold values from -0.375 to 0.375
- link_self_weight: bfloat16 [256, 256], replicated, may hold values from -0.375 to 0.375
- link_out_weight: bfloat16 [256, 256], replicated, may hold values from -0.375 to 0.375
- flow_gain: float32 [256], replicated, may hold values from 0.5 to 2
- flow_agg_weight: bfloat16 [256, 256], replicated, may hold values from -0.375 to 0.375
- flow_self_weight: bfloat16 [256, 256], replicated, may hold values from -0.375 to 0.375
- flow_out_weight: bfloat16 [256, 256], replicated, may hold values from -0.375 to 0.375
Outputs:
- link_next: bfloat16 [65536, 256], P(('row', 'col'))
- flow_next: bfloat16 [131072, 256], P(('col', 'row'))
Inputs may be any that keep to these rules, and one draw needn't show every extreme that they name: `tile_live`: in every draw some group pair has all 24 slots live; the number of live slots differs from pair to pair.
All inputs are finite; a program needn't handle non-finite values.
Results may differ from a plain program's by a relative error of at most 0.018.
Values may be sent and summed in bfloat16 or wider, within the bound.
No kernel may reach another device: no remote copies, remote signals or barrier semaphores. Data moves between devices by JAX's collectives and lax.ppermute only.
A program may use at most 64 MiB of HBM per device.

v0:
```python
import jax
import jax.numpy as jnp
from jax import lax
from jax.sharding import PartitionSpec as P

H = 256
BS = 128


def state_update(totals, state, gain, agg_weight, self_weight, out_weight):
    scale = lax.rsqrt(jnp.mean(totals * totals, axis=-1, keepdims=True) + 1e-05)
    normed = (totals * scale * gain).astype(jnp.bfloat16)
    before = jnp.dot(normed, agg_weight, preferred_element_type=jnp.float32) + jnp.dot(
        state, self_weight, preferred_element_type=jnp.float32
    )
    hidden = jax.nn.silu(before).astype(jnp.bfloat16)
    return (
        state.astype(jnp.float32) + jnp.dot(hidden, out_weight, preferred_element_type=jnp.float32)
    ).astype(jnp.bfloat16)


def selector(targets, live_slots, block_count):
    select = (targets[None, :] == jnp.arange(block_count, dtype=jnp.int32)[:, None]).astype(
        jnp.float32
    )
    return select * live_slots.astype(jnp.float32)[None, :]


def on_device(
    flow_state,
    link_state,
    incidence,
    tile_flow,
    tile_link,
    tile_live,
    link_gain,
    link_agg_weight,
    link_self_weight,
    link_out_weight,
    flow_gain,
    flow_agg_weight,
    flow_self_weight,
    flow_out_weight,
):
    coefs = incidence[0, 0]
    flow_slots = tile_flow[0, 0]
    link_slots = tile_link[0, 0]
    live_slots = tile_live[0, 0]
    slot_count = coefs.shape[0]
    flow_blocks_here = flow_state.shape[0] // BS
    link_blocks_here = link_state.shape[0] // BS
    link_blocks = link_blocks_here * lax.axis_size("col")
    flow_group = lax.all_gather(flow_state, "row", axis=0, tiled=True)
    flow_blocks = flow_group.shape[0] // BS
    flow_pieces = jnp.take(flow_group.reshape(flow_blocks, BS, H), flow_slots, axis=0)
    link_terms = jnp.einsum(
        "tij,tih->tjh", coefs, flow_pieces, preferred_element_type=jnp.float32
    ).reshape(slot_count, BS * H)
    link_select = selector(link_slots, live_slots, link_blocks)
    chosen = link_select
    link_sum = lax.psum_scatter(
        jnp.dot(chosen, link_terms, precision=lax.Precision.HIGHEST).astype(jnp.bfloat16),
        "col",
        scatter_dimension=0,
        tiled=True,
    ).astype(jnp.float32)
    link_next = state_update(
        link_sum.reshape(link_blocks_here * BS, H),
        link_state,
        link_gain,
        link_agg_weight,
        link_self_weight,
        link_out_weight,
    )
    link_group = lax.all_gather(link_next, "col", axis=0, tiled=True)
    link_pieces = jnp.take(link_group.reshape(link_blocks, BS, H), link_slots, axis=0)
    flow_terms = jnp.einsum(
        "tij,tjh->tih", coefs, link_pieces, preferred_element_type=jnp.float32
    ).reshape(slot_count, BS * H)
    flow_select = selector(flow_slots, live_slots, flow_blocks)
    chosen = flow_select
    flow_sum = lax.psum_scatter(
        jnp.dot(chosen, flow_terms, precision=lax.Precision.HIGHEST).astype(jnp.bfloat16),
        "row",
        scatter_dimension=0,
        tiled=True,
    ).astype(jnp.float32)
    flow_next = state_update(
        flow_sum.reshape(flow_blocks_here * BS, H),
        flow_state,
        flow_gain,
        flow_agg_weight,
        flow_self_weight,
        flow_out_weight,
    )
    return (link_next, flow_next)


def solution(mesh):
    return jax.shard_map(
        on_device,
        mesh=mesh,
        in_specs=(
            P(("col", "row"), None),
            P(("row", "col"), None),
            P("row", "col", None, None, None),
            P("row", "col", None),
            P("row", "col", None),
            P("row", "col", None),
            P(),
            P(),
            P(),
            P(),
            P(),
            P(),
            P(),
            P(),
        ),
        out_specs=(P(("row", "col"), None), P(("col", "row"), None)),
        check_vma=False,
    )
```

profile of v0, /device:TPU:2, one launch (start us, length us, event | category | flops | bytes accessed | tf_op | source)
XLA Modules:
  0.0 468.4 jit_solution(17944627231696059716)
XLA Ops:
  7.2 0.7 all-gather.3.cloned.1.call-update
  8.0 0.7 compare_select_fusion.1
  8.6 0.7 compare_and_fusion.1
  9.3 0.7 convert_bitcast_fusion
  9.9 77.7 %all-gather.3.cloned.1.call-done = bf16[4096,256]{1,0:T(8,128)(2,1)} async-done(((bf16[256,256]{1,0:T(8,128)(2,1)}), bf16[4096,256]{1,0:T(8,128)(2,1)}) %all-gather.3.cloned.1.call-update) | async-done | bytes 2097168 | tf_op jit(solution)/shard_map/all_gather | solution.py:53
  87.7 2.2 gather_fusion
  89.9 2.4 convolution_bitcast_fusion.1
  92.3 3.6 copy.26
  95.9 6.7 %convolution_convert_fusion.1 = bf16[32,32768]{1,0:T(8,128)(2,1)} fusion(f32[24,32768]{1,0:T(8,128)} %bitcast.40, f32[24]{0:T(128)S(1)} %convert_bitcast_fusion, s32[24]{0:T(128)S(1)} %bitcast.45), kind=kOutput, calls=%fused_computation.3 | convolution fusion | flops 303040000 | bytes 5243072 | tf_op jit(solution)/shard_map/dot_general | solution.py:62
  102.6 1.4 dynamic-slice
  104.0 133.2 %all-reduce.5.cloned.1.call-done = bf16[32,32768]{1,0:T(8,128)(2,1)} async-done(((bf16[32,32768]{1,0:T(8,128)(2,1)}), bf16[32,32768]{1,0:T(8,128)(2,1)}) %all-reduce.5.cloned.1.call-update) | async-done | bytes 2097168
  237.2 2.1 fusion.11
  239.7 0.9 fusion.5
  240.8 59.3 %all-gather.5.cloned.1.call-done = bf16[4096,256]{1,0:T(8,128)(2,1)} async-done(((bf16[128,256]{1,0:T(8,128)(2,1)}), bf16[4096,256]{1,0:T(8,128)(2,1)}) %all-gather.5.cloned.1.call-update) | async-done | bytes 2097168 | tf_op jit(solution)/shard_map/all_gather | solution.py:75
  300.1 2.2 gather_fusion.1
  302.3 2.4 convolution_bitcast_fusion
  304.7 3.6 copy.27
  308.3 6.7 %convolution_convert_fusion = bf16[32,32768]{1,0:T(8,128)(2,1)} fusion(f32[24,32768]{1,0:T(8,128)} %bitcast.39, s32[24]{0:T(128)S(1)} %bitcast.46, f32[24]{0:T(128)S(1)} %convert_bitcast_fusion), kind=kOutput, calls=%fused_computation.2 | convolution fusion | flops 303040000 | bytes 5243072 | tf_op jit(solution)/shard_map/dot_general | solution.py:83
  315.0 1.4 dynamic-slice.2
  317.0 142.1 %all-reduce.7.cloned.1.call-done = bf16[32,32768]{1,0:T(8,128)(2,1)} async-done(((bf16[32,32768]{1,0:T(8,128)(2,1)}), bf16[32,32768]{1,0:T(8,128)(2,1)}) %all-reduce.7.cloned.1.call-update) | async-done | bytes 2097168
  459.0 1.1 dynamic-slice_convert_fusion
  460.2 0.2 reshape.70
  460.6 0.2 fusion.10
  460.8 1.0 fusion.4
  (43 shorter events, 0.8 us)
Async XLA Ops:
  7.2 82.8 %copy-start = (bf16[1,1,24,128,128]{4,3,2,1,0:T(8,128)(2,1)S(1)}, bf16[1,1,24,128,128]{4,3,2,1,0:T(8,128)(2,1)}, u32[]{:S(2)}) copy-start(bf16[1,1,24,128,128]{4,3,2,1,0:T(8,128)(2,1)} %param.18) | copy-start | bytes 2359300
  7.2 80.5 %all-gather.3.cloned.1.call-start = ((), (), s32[]{:S(2)}) async-start(), calls=%async_computation | async-start | bytes 2228224 | tf_op jit(solution)/shard_map/all_gather | solution.py:53
  7.9 229.3 %all-reduce.5.cloned.1.call-start = ((), (), s32[]{:S(2)}) async-start(), calls=%async_computation.2 | async-start | bytes 4194304
  92.3 3.6 copy-start.6
  102.5 136.9 %copy-start.2 = (bf16[256,256]{1,0:T(8,128)(2,1)S(1)}, bf16[256,256]{1,0:T(8,128)(2,1)}, u32[]{:S(2)}) copy-start(bf16[256,256]{1,0:T(8,128)(2,1)} %param.23) | copy-start | bytes 393220
  102.5 137.0 %copy-start.4 = (f32[256]{0:T(256)S(1)}, f32[256]{0:T(256)}, u32[]{:S(2)}) copy-start(f32[256]{0:T(256)} %param.22) | copy-start | bytes 3076
  102.5 137.2 %copy-start.8 = (bf16[256,256]{1,0:T(8,128)(2,1)S(1)}, bf16[256,256]{1,0:T(8,128)(2,1)}, u32[]{:S(2)}) copy-start(bf16[256,256]{1,0:T(8,128)(2,1)} %param.25) | copy-start | bytes 393220
  102.5 137.2 %copy-start.9 = (bf16[256,256]{1,0:T(8,128)(2,1)S(1)}, bf16[256,256]{1,0:T(8,128)(2,1)}, u32[]{:S(2)}) copy-start(bf16[256,256]{1,0:T(8,128)(2,1)} %param.24) | copy-start | bytes 393220
  102.5 137.2 %copy-start.12 = (bf16[128,256]{1,0:T(8,128)(2,1)S(1)}, bf16[128,256]{1,0:T(8,128)(2,1)}, u32[]{:S(2)}) copy-start(bf16[128,256]{1,0:T(8,128)(2,1)} %param.17) | copy-start | bytes 196612
  102.6 197.5 %all-gather.5.cloned.1.call-start = ((), (), s32[]{:S(2)}) async-start(), calls=%async_computation.1 | async-start | bytes 2162688 | tf_op jit(solution)/shard_map/all_gather | solution.py:75
  240.7 218.3 %all-reduce.7.cloned.1.call-start = ((), (), s32[]{:S(2)}) async-start(), calls=%async_computation.3 | async-start | bytes 4194304
  304.7 3.6 copy-start.7
  314.9 145.6 %copy-start.1 = (bf16[256,256]{1,0:T(8,128)(2,1)S(1)}, bf16[256,256]{1,0:T(8,128)(2,1)}, u32[]{:S(2)}) copy-start(bf16[256,256]{1,0:T(8,128)(2,1)} %param.27) | copy-start | bytes 393220
  314.9 145.6 %copy-start.5 = (f32[256]{0:T(256)S(1)}, f32[256]{0:T(256)}, u32[]{:S(2)}) copy-start(f32[256]{0:T(256)} %param.26) | copy-start | bytes 3076
  314.9 145.9 %copy-start.3 = (bf16[256,256]{1,0:T(8,128)(2,1)S(1)}, bf16[256,256]{1,0:T(8,128)(2,1)}, u32[]{:S(2)}) copy-start(bf16[256,256]{1,0:T(8,128)(2,1)} %param.16) | copy-start | bytes 393220
  314.9 145.9 %copy-start.10 = (bf16[256,256]{1,0:T(8,128)(2,1)S(1)}, bf16[256,256]{1,0:T(8,128)(2,1)}, u32[]{:S(2)}) copy-start(bf16[256,256]{1,0:T(8,128)(2,1)} %param.29) | copy-start | bytes 393220
  314.9 145.9 %copy-start.11 = (bf16[256,256]{1,0:T(8,128)(2,1)S(1)}, bf16[256,256]{1,0:T(8,128)(2,1)}, u32[]{:S(2)}) copy-start(bf16[256,256]{1,0:T(8,128)(2,1)} %param.28) | copy-start | bytes 393220
Sparse Core Ops, SparseCore 0:
  10.1 77.5 all-gather.2
  102.7 134.4 all-reduce.4
  240.9 59.1 all-gather.4
  315.1 143.8 all-reduce.6
where the time goes:
time: 469 us; the launch traced here: 468 us
  waiting for transfers between devices  413 us (88%)
  matrix products  20.5 us (4%)
  local copies, waits for them, and re-layouts  14.7 us (3%)
  between operations  14.6 us (3%)
  other arithmetic  5.46 us (1%)
    unnamed x6, waiting for transfers between devices  276 us
    all_gather x1, waiting for transfers between devices, on_device(): flow_group = lax.all_gather(flow_state, 'row', axis=0, tiled=True)  77.7 us
    all_gather x1, waiting for transfers between devices, on_device(): link_group = lax.all_gather(link_next, 'col', axis=0, tiled=True)  59.3 us
    unnamed x30, local copies, waits for them, and re-layouts  9.94 us
  transfers between devices with their start and end apart: 4, of which 4 were waited for; matrix products, arithmetic and copies ran while one was open for 1% of the time, Pallas kernels for 0%

commit v1 on v0

--- a/solution.py
+++ b/solution.py
@@ -5,6 +5,11 @@
 
 H = 256
 BS = 128
+
+
+def gather_from_all(value, axis, dim):
+    copies = jnp.concatenate([value] * lax.axis_size(axis), axis=dim)
+    return lax.all_to_all(copies, axis, dim, dim, tiled=True)
 
 
 def state_update(totals, state, gain, agg_weight, self_weight, out_weight):
@@ -72,7 +77,7 @@
         link_self_weight,
         link_out_weight,
     )
-    link_group = lax.all_gather(link_next, "col", axis=0, tiled=True)
+    link_group = gather_from_all(link_next, "col", 0)
     link_pieces = jnp.take(link_group.reshape(link_blocks, BS, H), link_slots, axis=0)
     flow_terms = jnp.einsum(
         "tij,tjh->tih", coefs, link_pieces, preferred_element_type=jnp.float32

time: 469 us -> 445 us (0.949)
  waiting for transfers between devices: 413 us -> 381 us
  starting transfers between devices: 0.16 us -> 6.75 us
    all_gather x1 -> x0, waiting for transfers between devices: 59.3 us -> none  [on_device(): link_group = lax.all_gather(link_next, 'col', axis=0, tiled=True)]
    all_to_all x0 -> x1, waiting for transfers between devices: none -> 27.6 us  [gather_from_all(): return lax.all_to_all(copies, axis, dim, dim, tiled=True)]
    all_to_all x0 -> x1, starting transfers between devices: none -> 6.45 us  [gather_from_all(): return lax.all_to_all(copies, axis, dim, dim, tiled=True)]
    unnamed x30 -> x64, local copies, waits for them, and re-layouts: 9.94 us -> 11.5 us
    unnamed x6 -> x5, waiting for transfers between devices: 276 us -> 275 us
where the time goes in v1:
time: 445 us
  waiting for transfers between devices  381 us (86%)
  matrix products  21.2 us (5%)
  local copies, waits for them, and re-layouts  15.8 us (4%)
  between operations  14.9 us (3%)
  starting transfers between devices  6.75 us (2%)
  other arithmetic  5.46 us (1%)
    unnamed x5, waiting for transfers between devices  275 us
    all_gather x1, waiting for transfers between devices, on_device(): flow_group = lax.all_gather(flow_state, 'row', axis=0, tiled=True)  77.7 us
    all_to_all x1, waiting for transfers between devices, gather_from_all(): return lax.all_to_all(copies, axis, dim, dim, tiled=True)  27.6 us
    unnamed x64, local copies, waits for them, and re-layouts  11.5 us
  transfers between devices with their start and end apart: 4, of which 4 were waited for; matrix products, arithmetic and copies ran while one was open for 1% of the time, Pallas kernels for 0%

profile of v1, /device:TPU:2, one launch (start us, length us, event | category | flops | bytes accessed | tf_op | source)
XLA Modules:
  0.0 444.9 jit_solution(8017659849406293421)
XLA Ops:
  7.2 0.7 all-gather.2.cloned.1.call-update
  8.0 0.7 compare_select_fusion.1
  8.6 0.7 compare_and_fusion.1
  9.3 0.7 convert_bitcast_fusion
  9.9 77.7 %all-gather.2.cloned.1.call-done = bf16[4096,256]{1,0:T(8,128)(2,1)} async-done(((bf16[256,256]{1,0:T(8,128)(2,1)}), bf16[4096,256]{1,0:T(8,128)(2,1)}) %all-gather.2.cloned.1.call-update) | async-done | bytes 2097168 | tf_op jit(solution)/shard_map/all_gather | solution.py:58
  87.7 2.2 gather_fusion
  89.9 2.4 convolution_bitcast_fusion.1
  92.3 3.6 copy.26
  95.9 6.7 %convolution_convert_fusion.1 = bf16[32,32768]{1,0:T(8,128)(2,1)} fusion(f32[24,32768]{1,0:T(8,128)} %bitcast.40, f32[24]{0:T(128)S(1)} %convert_bitcast_fusion, s32[24]{0:T(128)S(1)} %bitcast.45), kind=kOutput, calls=%fused_computation.3 | convolution fusion | flops 303040000 | bytes 5243072 | tf_op jit(solution)/shard_map/dot_general | solution.py:67
  102.6 1.4 dynamic-slice
  104.0 133.3 %all-reduce.5.cloned.1.call-done = bf16[32,32768]{1,0:T(8,128)(2,1)} async-done(((bf16[32,32768]{1,0:T(8,128)(2,1)}), bf16[32,32768]{1,0:T(8,128)(2,1)}) %all-reduce.5.cloned.1.call-update) | async-done | bytes 2097168
  237.3 2.1 fusion.11
  239.8 0.3 constant_dynamic-update-slice_fusion.31
  240.6 1.3 copy-done.2
  241.9 6.5 %all-to-all-start = ((bf16[32,128,256]{2,1,0:T(8,128)(2,1)}), bf16[32,128,256]{2,1,0:T(8,128)(2,1)S(1)}, u32[]{:S(2)}, u32[]{:S(2)}) async-start(bf16[32,128,256]{2,1,0:T(8,128)(2,1)} %bitcast.43), calls=%async_computation | async-start | bytes 4194304 | tf_op jit(solution)/shard_map/all_to_all | solution.py:12
  248.6 27.6 %all-to-all-done = bf16[32,128,256]{2,1,0:T(8,128)(2,1)S(1)} async-done(((bf16[32,128,256]{2,1,0:T(8,128)(2,1)}), bf16[32,128,256]{2,1,0:T(8,128)(2,1)S(1)}, u32[]{:S(2)}, u32[]{:S(2)}) %all-to-all-start) | async-done | bytes 2097184 | tf_op jit(solution)/shard_map/all_to_all | solution.py:12
  276.2 1.8 gather_fusion.1
  278.1 3.7 convolution_bitcast_fusion
  281.8 3.6 copy.27
  285.4 6.6 %convolution_convert_fusion = bf16[32,32768]{1,0:T(8,128)(2,1)} fusion(f32[24,32768]{1,0:T(8,128)} %bitcast.39, s32[24]{0:T(128)S(1)} %bitcast.46, f32[24]{0:T(128)S(1)} %convert_bitcast_fusion), kind=kOutput, calls=%fused_computation.2 | convolution fusion | flops 303040000 | bytes 5243072 | tf_op jit(solution)/shard_map/dot_general | solution.py:88
  292.1 1.4 dynamic-slice.2
  294.1 141.4 %all-reduce.7.cloned.1.call-done = bf16[32,32768]{1,0:T(8,128)(2,1)} async-done(((bf16[32,32768]{1,0:T(8,128)(2,1)}), bf16[32,32768]{1,0:T(8,128)(2,1)}) %all-reduce.7.cloned.1.call-update) | async-done | bytes 2097168
  435.5 1.1 dynamic-slice_convert_fusion
  437.3 1.0 fusion.4
  (77 shorter events, 1.6 us)
Async XLA Ops:
  7.2 82.8 %copy-start = (bf16[1,1,24,128,128]{4,3,2,1,0:T(8,128)(2,1)S(1)}, bf16[1,1,24,128,128]{4,3,2,1,0:T(8,128)(2,1)}, u32[]{:S(2)}) copy-start(bf16[1,1,24,128,128]{4,3,2,1,0:T(8,128)(2,1)} %param.18) | copy-start | bytes 2359300
  7.2 80.5 %all-gather.2.cloned.1.call-start = ((), (), s32[]{:S(2)}) async-start(), calls=%async_computation.1 | async-start | bytes 2228224 | tf_op jit(solution)/shard_map/all_gather | solution.py:58
  7.9 229.3 %all-reduce.5.cloned.1.call-start = ((), (), s32[]{:S(2)}) async-start(), calls=%async_computation.2 | async-start | bytes 4194304
  92.3 3.6 copy-start.8
  102.5 137.0 %copy-start.4 = (bf16[256,256]{1,0:T(8,128)(2,1)S(1)}, bf16[256,256]{1,0:T(8,128)(2,1)}, u32[]{:S(2)}) copy-start(bf16[256,256]{1,0:T(8,128)(2,1)} %param.23) | copy-start | bytes 393220
  102.5 137.0 %copy-start.6 = (f32[256]{0:T(256)S(1)}, f32[256]{0:T(256)}, u32[]{:S(2)}) copy-start(f32[256]{0:T(256)} %param.22) | copy-start | bytes 3076
  102.6 137.2 %copy-start.10 = (bf16[256,256]{1,0:T(8,128)(2,1)S(1)}, bf16[256,256]{1,0:T(8,128)(2,1)}, u32[]{:S(2)}) copy-start(bf16[256,256]{1,0:T(8,128)(2,1)} %param.25) | copy-start | bytes 393220
  102.6 137.2 %copy-start.11 = (bf16[256,256]{1,0:T(8,128)(2,1)S(1)}, bf16[256,256]{1,0:T(8,128)(2,1)}, u32[]{:S(2)}) copy-start(bf16[256,256]{1,0:T(8,128)(2,1)} %param.24) | copy-start | bytes 393220
  102.6 137.2 %copy-start.14 = (bf16[128,256]{1,0:T(8,128)(2,1)S(1)}, bf16[128,256]{1,0:T(8,128)(2,1)}, u32[]{:S(2)}) copy-start(bf16[128,256]{1,0:T(8,128)(2,1)} %param.17) | copy-start | bytes 196612
  240.1 1.8 copy-start.1
  240.6 1.3 copy-start.2
  241.9 34.3 %all-to-all-start = ((bf16[32,128,256]{2,1,0:T(8,128)(2,1)}), bf16[32,128,256]{2,1,0:T(8,128)(2,1)S(1)}, u32[]{:S(2)}, u32[]{:S(2)}) async-start(bf16[32,128,256]{2,1,0:T(8,128)(2,1)} %bitcast.43), calls=%async_computation | async-start | bytes 4194304 | tf_op jit(solution)/shard_map/all_to_all | solution.py:12
  248.4 187.2 %all-reduce.7.cloned.1.call-start = ((), (), s32[]{:S(2)}) async-start(), calls=%async_computation.3 | async-start | bytes 4194304
  281.8 3.6 copy-start.9
  292.0 145.0 %copy-start.3 = (bf16[256,256]{1,0:T(8,128)(2,1)S(1)}, bf16[256,256]{1,0:T(8,128)(2,1)}, u32[]{:S(2)}) copy-start(bf16[256,256]{1,0:T(8,128)(2,1)} %param.27) | copy-start | bytes 393220
  292.0 145.0 %copy-start.7 = (f32[256]{0:T(256)S(1)}, f32[256]{0:T(256)}, u32[]{:S(2)}) copy-start(f32[256]{0:T(256)} %param.26) | copy-start | bytes 3076
  292.0 145.3 %copy-start.5 = (bf16[256,256]{1,0:T(8,128)(2,1)S(1)}, bf16[256,256]{1,0:T(8,128)(2,1)}, u32[]{:S(2)}) copy-start(bf16[256,256]{1,0:T(8,128)(2,1)} %param.16) | copy-start | bytes 393220
  292.0 145.3 %copy-start.12 = (bf16[256,256]{1,0:T(8,128)(2,1)S(1)}, bf16[256,256]{1,0:T(8,128)(2,1)}, u32[]{:S(2)}) copy-start(bf16[256,256]{1,0:T(8,128)(2,1)} %param.29) | copy-start | bytes 393220
  292.0 145.3 %copy-start.13 = (bf16[256,256]{1,0:T(8,128)(2,1)S(1)}, bf16[256,256]{1,0:T(8,128)(2,1)}, u32[]{:S(2)}) copy-start(bf16[256,256]{1,0:T(8,128)(2,1)} %param.28) | copy-start | bytes 393220
Sparse Core Ops, SparseCore 0:
  10.1 77.5 all-gather.1
  102.7 134.4 all-reduce.4
  292.2 143.2 all-reduce.6
